TPU v7x, 32 devices: a whole 2x2x4 slice. The times are simulated.
32 devices in a mesh: lat: 4 (over z), lon: 8 (over y, x, core).
Axes of the slice: x: 2, y: 2, z: 4, core: 2. Of those that a mesh axis runs over, the one named last changes fastest.
Arguments:
- latents: bfloat16 [64, 128, 256], P('lat', 'lon'), may hold values from -6 to 6
- conv_weight: bfloat16 [9, 256, 256], replicated, may hold values from -0.125 to 0.125
- map_weight: bfloat16 [256, 1024], replicated, may hold values from -0.375 to 0.375
- map_bias: float32 [1024], replicated, may hold values from -6 to 6
- input_weight: float32 [3, 512], replicated, may hold values from -3.5 to 3.5
- hidden_weight: bfloat16 [1, 512, 512], replicated, may hold values from -0.25 to 0.25
- output_weight: float32 [512], replicated, may hold values from -0.25 to 0.25
- hit_owner: int32 [768], P(('lat', 'lon')), may hold values from 0 to 31, as said below
- serve_block: int32 [32, 32], P(('lat', 'lon')), may hold values from -1 to 1, as said below
- query_grid: int32 [3, 49152], P(None, ('lat', 'lon')), may hold values from 0 to 127, as said below
- cotangent: float32 [49152], P(('lat', 'lon')), may hold values from -6 to 6
Outputs:
- latent_grad: float32 [64, 128, 256], P('lat', 'lon')
- conv_grad: float32 [9, 256, 256], replicated
- map_grad: float32 [256, 1024], replicated
- map_bias_grad: float32 [1024], replicated
- input_grad: float32 [3, 512], replicated
- hidden_grad: float32 [1, 512, 512], replicated
- output_grad: float32 [512], replicated
Inputs may be any that keep to these rules, and one draw needn't show every extreme that they name: `hit_owner`: each device's 24 entries name distinct devices, numbered lat index times the size of lon plus lon index. `serve_block`: entry [o, r] is a block of device o, 0 to 1, when the list of device r names o, and -1 otherwise. `query_grid`: row 0 is the cell within the block (row-major over 8 rows of 16 cells), row 1 the sub-cell (0 to 35, row-major), row 2 the level (0 to 36).
All inputs are finite; a program needn't handle non-finite values.
Results may differ from a plain program's by a relative error of at most 0.0095.
Values may be sent and summed in bfloat16 or wider, within the bound.
No kernel may reach another device: no remote copies, remote signals or barrier semaphores. Data moves between devices by JAX's collectives and lax.ppermute only.
A program may use at most 128 MiB of HBM per device.

v0:
```python
import jax
import jax.numpy as jnp
from jax import lax
from jax.sharding import PartitionSpec as P

BLOCK = 128
LEVELS = 37
SUB = 6


OMEGA = 30.0


def padded_2(block, sides, width):
    for axis, dim in sides:
        count = lax.axis_size(axis)
        forward = [(i, i + 1) for i in range(count - 1)]
        forward.append((count - 1, 0))
        backward = [(target, source) for source, target in forward]
        low = lax.ppermute(
            lax.slice_in_dim(block, block.shape[dim] - width, None, axis=dim), axis, forward
        )
        high = lax.ppermute(lax.slice_in_dim(block, 0, width, axis=dim), axis, backward)
        block = jnp.concatenate([low, block, high], axis=dim)
    return block


def conv_apply(padded, kernel, row_count, col_count, flipped):
    channels = padded.shape[-1]
    result = jnp.zeros((row_count * col_count, kernel.shape[-1]), jnp.float32)
    for shift_a in (-1, 0, 1):
        for shift_b in (-1, 0, 1):
            tap_index = (shift_a + 1) * 3 + shift_b + 1
            if flipped:
                window = padded[
                    1 - shift_a : 1 - shift_a + row_count, 1 - shift_b : 1 - shift_b + col_count
                ]
                matrix = kernel[tap_index].T
            else:
                window = padded[
                    1 + shift_a : 1 + shift_a + row_count, 1 + shift_b : 1 + shift_b + col_count
                ]
                matrix = kernel[tap_index]
            result = result + jnp.dot(
                window.reshape(row_count * col_count, channels),
                matrix,
                preferred_element_type=jnp.float32,
            )
    return result


def conv_weight_grad(padded, grads, row_count, col_count):
    flat_grads = grads.reshape(row_count * col_count, -1)
    pieces = []
    for shift_a in (-1, 0, 1):
        for shift_b in (-1, 0, 1):
            window = padded[
                1 + shift_a : 1 + shift_a + row_count, 1 + shift_b : 1 + shift_b + col_count
            ]
            window = window.reshape(row_count * col_count, -1)
            pieces.append(jnp.dot(window.T, flat_grads, preferred_element_type=jnp.float32))
    return jnp.stack(pieces)


def close_poles(padded, lat_pos, lat_parts):
    top_rim = jnp.where(lat_pos == 0, jnp.zeros_like(padded[:1]), padded[:1])
    bottom_rim = jnp.where(lat_pos == lat_parts - 1, jnp.zeros_like(padded[-1:]), padded[-1:])
    return jnp.concatenate([top_rim, padded[1:-1], bottom_rim], axis=0)


def split_parts(values):
    upper = values.astype(jnp.bfloat16)
    lower = (values - upper.astype(jnp.float32)).astype(jnp.bfloat16)
    return (upper, lower)


def query_coords(
    cell_index, sub_index, level_index, lat_base, lon_base, lon_tile, lat_cells, lon_cells
):
    row_index = lat_base[:, None] + cell_index // lon_tile
    col_index = lon_base[:, None] + cell_index % lon_tile
    lat_coord = ((row_index * SUB + sub_index // SUB).astype(jnp.float32) + 0.5) / (
        lat_cells * SUB
    ) * 2.0 - 1.0
    lon_coord = ((col_index * SUB + sub_index % SUB).astype(jnp.float32) + 0.5) / (
        lon_cells * SUB
    ) * 2.0 - 1.0
    level_coord = (level_index.astype(jnp.float32) + 0.5) / LEVELS * 2.0 - 1.0
    return jnp.stack([lat_coord.reshape(-1), lon_coord.reshape(-1), level_coord.reshape(-1)])


def sine_grads(
    features, coords, cotan_rows, map_weight, map_bias, input_weight, hidden_weight, output_weight
):
    hidden_size = input_weight.shape[1]
    depth_count = map_weight.shape[1] // hidden_size
    shifts = jnp.dot(features, map_weight, preferred_element_type=jnp.float32) + map_bias
    linear = (
        coords[0][:, None] * input_weight[0]
        + coords[1][:, None] * input_weight[1]
        + coords[2][:, None] * input_weight[2]
    )
    preacts = [OMEGA * linear + shifts[:, :hidden_size]]
    layer_index = 1
    previous = jnp.sin(preacts[-1]).astype(jnp.bfloat16)
    inputs_rounded = [previous]
    preacts.append(
        jnp.dot(previous, hidden_weight[layer_index - 1], preferred_element_type=jnp.float32)
        + shifts[:, layer_index * hidden_size : (layer_index + 1) * hidden_size]
    )
    last_act = jnp.sin(preacts[-1])
    output_grad = jnp.dot(cotan_rows, last_act, precision=lax.Precision.HIGHEST)
    act_grad = cotan_rows[:, None] * output_weight[None, :]
    pre_grads = [None] * depth_count
    rounded_grads = [None] * depth_count
    hidden_grads = [None] * (depth_count - 1)
    for layer_index in range(depth_count - 1, -1, -1):
        pre_grads[layer_index] = act_grad * jnp.cos(preacts[layer_index])
        rounded_grads[layer_index] = pre_grads[layer_index].astype(jnp.bfloat16)
        if layer_index > 0:
            hidden_grads[layer_index - 1] = jnp.dot(
                inputs_rounded[layer_index - 1].T,
                rounded_grads[layer_index],
                preferred_element_type=jnp.float32,
            )
            act_grad = jnp.dot(
                rounded_grads[layer_index],
                hidden_weight[layer_index - 1].T,
                preferred_element_type=jnp.float32,
            )
    input_grad = OMEGA * jnp.dot(coords, pre_grads[0], precision=lax.Precision.HIGHEST)
    mod_grads = jnp.concatenate(rounded_grads, axis=1)
    bias_grad = jnp.sum(jnp.concatenate(pre_grads, axis=1), axis=0)
    map_grad = jnp.dot(features.T, mod_grads, preferred_element_type=jnp.float32)
    feature_grads = jnp.dot(mod_grads, map_weight.T, preferred_element_type=jnp.float32)
    return (feature_grads, (map_grad, bias_grad, input_grad, jnp.stack(hidden_grads), output_grad))


def run_groups(
    blocks,
    cell_index,
    sub_index,
    level_index,
    lat_base,
    lon_base,
    cotan_rows,
    weights,
    lon_tile,
    lat_cells,
    lon_cells,
):
    group_count = blocks.shape[0]
    block_rows = blocks.shape[1]
    channels = blocks.shape[2]
    step_size = 8
    turns = group_count // step_size

    def split_turns(source):
        return source.reshape((turns, step_size) + source.shape[1:])

    inputs = (
        split_turns(blocks),
        split_turns(cell_index),
        split_turns(sub_index),
        split_turns(level_index),
        split_turns(lat_base),
        split_turns(lon_base),
        split_turns(cotan_rows),
    )
    map_weight, map_bias, input_weight, hidden_weight, output_weight = weights
    initial = (
        jnp.zeros(map_weight.shape, jnp.float32),
        jnp.zeros(map_bias.shape, jnp.float32),
        jnp.zeros(input_weight.shape, jnp.float32),
        jnp.zeros(hidden_weight.shape, jnp.float32),
        jnp.zeros(output_weight.shape, jnp.float32),
    )

    def advance(grad_totals, slices):
        block_part, cell_part, sub_part, level_part, latb_part, lonb_part, cotan_part = slices
        onehot = (
            cell_part[:, :, None] == jnp.arange(block_rows, dtype=jnp.int32)[None, None, :]
        ).astype(jnp.bfloat16)
        features_q = jnp.einsum(
            "hgb,hbc->hgc", onehot, block_part, preferred_element_type=jnp.float32
        ).astype(jnp.bfloat16)
        coords = query_coords(
            cell_part, sub_part, level_part, latb_part, lonb_part, lon_tile, lat_cells, lon_cells
        )
        feature_grads, grads = sine_grads(
            features_q.reshape(-1, channels),
            coords,
            cotan_part.reshape(-1),
            map_weight,
            map_bias,
            input_weight,
            hidden_weight,
            output_weight,
        )
        upper, lower = split_parts(
            feature_grads.reshape(onehot.shape[0], onehot.shape[1], channels)
        )
        block_grads = jnp.einsum(
            "hgb,hgc->hbc", onehot, upper, preferred_element_type=jnp.float32
        ) + jnp.einsum("hgb,hgc->hbc", onehot, lower, preferred_element_type=jnp.float32)
        return (jax.tree.map(jnp.add, grad_totals, grads), block_grads)

    grad_totals, block_grads = lax.scan(advance, initial, inputs)
    return (block_grads.reshape(group_count, block_rows, channels), grad_totals)


def on_device(
    latents,
    conv_weight,
    map_weight,
    map_bias,
    input_weight,
    hidden_weight,
    output_weight,
    hit_owner,
    serve_block,
    query_grid,
    cotangent,
):
    lat_tile, lon_tile, channels = latents.shape
    lat_parts = lax.axis_size("lat")
    lon_parts = lax.axis_size("lon")
    dev_count = lat_parts * lon_parts
    lat_cells = lat_tile * lat_parts
    lon_cells = lon_tile * lon_parts
    block_rows = BLOCK
    tile_blocks = lat_tile * lon_tile // block_rows
    rows_per_block = block_rows // lon_tile
    lat_pos = lax.axis_index("lat")
    lon_pos = lax.axis_index("lon")
    padded = close_poles(padded_2(latents, (("lat", 0), ("lon", 1)), 1), lat_pos, lat_parts)
    features = conv_apply(padded, conv_weight, lat_tile, lon_tile, False).astype(jnp.bfloat16)
    own_blocks = features.reshape(tile_blocks, block_rows * channels)
    serve_row = serve_block[0]
    selector = (serve_row[:, None] == jnp.arange(tile_blocks, dtype=jnp.int32)[None, :]).astype(
        jnp.bfloat16
    )
    slot_blocks = jnp.dot(selector, own_blocks, preferred_element_type=jnp.float32).astype(
        jnp.bfloat16
    )
    slot_blocks = slot_blocks.reshape(dev_count, block_rows, channels)
    weights = (map_weight, map_bias, input_weight, hidden_weight, output_weight)
    hit_count = hit_owner.shape[0]
    group_size = cotangent.shape[0] // hit_count
    grid_groups = query_grid.reshape(3, hit_count, group_size).transpose(1, 0, 2)
    grid_slots = jnp.zeros((dev_count, 3, group_size), jnp.int32).at[hit_owner].set(grid_groups)
    cotan_slots = (
        jnp.zeros((dev_count, group_size), jnp.float32)
        .at[hit_owner]
        .set(cotangent.reshape(hit_count, group_size))
    )
    grid_in, cotan_in = (
        lax.all_to_all(grid_slots, ("lat", "lon"), split_axis=0, concat_axis=0, tiled=True),
        lax.all_to_all(cotan_slots, ("lat", "lon"), split_axis=0, concat_axis=0, tiled=True),
    )
    lat_base = lat_pos * lat_tile + serve_row * rows_per_block
    lon_base = jnp.zeros((dev_count,), jnp.int32) + lon_pos * lon_tile
    slot_grads, grad_totals = run_groups(
        slot_blocks,
        grid_in[:, 0],
        grid_in[:, 1],
        grid_in[:, 2],
        lat_base,
        lon_base,
        cotan_in,
        weights,
        lon_tile,
        lat_cells,
        lon_cells,
    )
    slot_upper, slot_lower = split_parts(slot_grads.reshape(dev_count, block_rows * channels))
    tile_grads = jnp.dot(selector.T, slot_upper, preferred_element_type=jnp.float32) + jnp.dot(
        selector.T, slot_lower, preferred_element_type=jnp.float32
    )
    feature_grad = tile_grads.reshape(lat_tile, lon_tile, channels).astype(jnp.bfloat16)
    padded_grad = close_poles(
        padded_2(feature_grad, (("lat", 0), ("lon", 1)), 1), lat_pos, lat_parts
    )
    latent_grad = conv_apply(padded_grad, conv_weight, lat_tile, lon_tile, True).reshape(
        lat_tile, lon_tile, channels
    )
    conv_local = conv_weight_grad(padded, feature_grad, lat_tile, lon_tile)
    totals = lax.psum(
        (
            conv_local,
            grad_totals[0],
            grad_totals[1],
            grad_totals[2],
            grad_totals[3],
            grad_totals[4],
        ),
        ("lat", "lon"),
    )
    grad_scale = float(hit_count * group_size * dev_count) ** (-0.5)
    return (
        latent_grad,
        totals[0] * grad_scale,
        totals[1] * grad_scale,
        totals[2] * grad_scale,
        totals[3] * grad_scale,
        totals[4] * grad_scale,
        totals[5] * grad_scale,
    )


def solution(mesh):
    placed = (
        P("lat", "lon", None),
        P(),
        P(),
        P(),
        P(),
        P(),
        P(),
        P(("lat", "lon")),
        P(("lat", "lon"), None),
        P(None, ("lat", "lon")),
        P(("lat", "lon")),
    )
    return jax.shard_map(
        on_device,
        mesh=mesh,
        in_specs=placed,
        out_specs=(P("lat", "lon", None), P(), P(), P(), P(), P(), P()),
        check_vma=False,
    )
```

profile of v0, /device:TPU:0, one launch (start us, length us, event | category | flops | bytes accessed | tf_op | source)
XLA Modules:
  0.0 379.6 jit_solution(5831723974505579724)
XLA Ops:
  8.0 5.1 %collective-permute-start.1 = (bf16[1,16,256]{2,1,0:T(8,128)(2,1)S(1)}, bf16[1,16,256]{2,1,0:T(8,128)(2,1)S(1)}, u32[]{:S(2)}, u32[]{:S(2)}) collective-permute-start(bf16[1,16,256]{2,1,0:T(8,128)(2,1)S(1)} %get-tuple-element.522), channel_id=1, source_target_pairs={{8,0},{16,8},{24,16},{0,24},{9,1},{17,9},{25,17},{1,25},{10,2},{18... | collective-permute-start | bytes 24584 | tf_op jit(solution)/shard_map/ppermute | solution.py:23
  14.6 1.6 scatter_fusion
  16.9 6.2 %all-to-all-start = ((s32[32,1,192]{2,1,0:T(1,128)}), s32[32,1,192]{2,1,0:T(1,128)}, u32[]{:S(2)}, u32[]{:S(2)}) async-start(s32[32,1,192]{2,1,0:T(1,128)} %reshape.659), calls=%async_computation | async-start | bytes 65536 | tf_op jit(solution)/shard_map/all_to_all | solution.py:258
  25.5 2.5 collective-permute-start.3
  32.9 2.1 convolution_convert_fusion.1
  34.9 4.9 %all-to-all-start.1 = ((f32[32,1,64]{2,1,0:T(1,128)}), f32[32,1,64]{2,1,0:T(1,128)S(1)}, u32[]{:S(2)}, u32[]{:S(2)}) async-start(f32[32,1,64]{2,1,0:T(1,128)} %bitcast.22), calls=%async_computation.1 | async-start | bytes 32768 | tf_op jit(solution)/shard_map/all_to_all | solution.py:259
  42.0 5.0 %all-to-all-done.1 = f32[32,1,64]{2,1,0:T(1,128)S(1)} async-done(((f32[32,1,64]{2,1,0:T(1,128)}), f32[32,1,64]{2,1,0:T(1,128)S(1)}, u32[]{:S(2)}, u32[]{:S(2)}) %all-to-all-start.1) | async-done | bytes 8224 | tf_op jit(solution)/shard_map/all_to_all | solution.py:259
  47.0 110.0 %while.24 = (s32[]{:T(128)}, f32[256,1024]{1,0:T(8,128)S(1)}, f32[1024]{0:T(1024)S(1)}, f32[3,512]{1,0:T(4,128)}, f32[1,512,512]{2,1,0:T(8,128)}, /*index=5*/f32...) while((s32[]{:T(128)}, f32[256,1024]{1,0:T(8,128)S(1)}, ...), condition=%wide.region_4.5_spmd.clone, body=%wide.region_2.4_spmd.clone.sunk | while | flops 1739577856 | bytes 41995484 | solution.py:208
  51.5 7.2 %fusion.204 = (bf16[512,512]{1,0:T(8,128)(2,1)S(1)}, f32[512,512]{1,0:T(8,128)S(1)}, f32[512,512]{1,0:T(8,128)S(1)}) fusion(f32[512]{0:T(512)S(1)} %copy-done.28, f32[512]{0:T(512)S(1)} %mul.582, f32[512,1024]{1,0:T(8,128)S(1)} %convolution_add_fusion.19, bf16[1,512,512]{2,1,0:T(8,128)(2,1)S(1)} %copy-done.27, f32[512]{0:T(512)S(1)} %bitcast.281, ...), kind=kOutput, calls=%fused_computation.233.clone.1 | convolution fusion | flops 271581184 | bytes 5259264 | tf_op jit(solution)/shard_map/while/body/eval_jaxpr/dot_general | solution.py:108
  58.6 4.0 %fusion.208 = f32[1,512]{1,0:T(1,128)S(1)} fusion(f32[512,1]{0,1:T(1,128)S(1)} %reshape.662, f32[512,512]{1,0:T(8,128)S(1)} %get-tuple-element.679), kind=kOutput, calls=%fused_computation.17.clone.1 | convolution fusion | flops 3145728 | bytes 1052672 | tf_op jit(solution)/shard_map/while/body/eval_jaxpr/dot_general | solution.py:112
  62.7 4.1 %fusion.207 = f32[1,512,512]{2,1,0:T(8,128)S(1)} fusion(bf16[512,512]{1,0:T(8,128)(2,1)S(1)} %get-tuple-element.673, f32[1,512,512]{2,1,0:T(8,128)S(1)} %copy-done.4, pred[]{:T(512)S(6)} %compare.35, f32[512,1024]{1,0:T(8,128)S(1)} %convolution_add_fusion.19, f32[512]{0:T(512)S(1)} %bitcast.282, f32[512]{0:T(512)S(1)} %sub.107, ...), kind=kOutput, calls=%fused_computation.11.clone.1 | convolution fusion | flops 271056896 | bytes 3682305 | tf_op jit(solution)/shard_map/while/body/eval_jaxpr/dot_general | solution.py:121
  66.8 3.8 %fusion.205 = (bf16[512,512]{1,0:T(8,128)(2,1)S(1)}, f32[512,512]{1,0:T(8,128)S(1)}) fusion(f32[512,1024]{1,0:T(8,128)S(1)} %convolution_add_fusion.19, f32[512]{0:T(512)S(1)} %bitcast.283, f32[512]{0:T(512)S(1)} %sub.107, f32[512]{0:T(512)S(1)} %bitcast.286, f32[512]{0:T(512)S(1)} %get-tuple-element.670, f32[512]{0:T(512)S(1)} %bitcast.280, ...), kind=kOutput, calls=%fused_computation.235.clone.1 | convolution fusion | flops 270794752 | bytes 3682304 | tf_op jit(solution)/shard_map/while/body/eval_jaxpr/dot_general | solution.py:126
  73.0 1.5 fusion.211
  79.0 7.2 %fusion.204 = (bf16[512,512]{1,0:T(8,128)(2,1)S(1)}, f32[512,512]{1,0:T(8,128)S(1)}, f32[512,512]{1,0:T(8,128)S(1)}) fusion(f32[512]{0:T(512)S(1)} %copy-done.28, f32[512]{0:T(512)S(1)} %mul.582, f32[512,1024]{1,0:T(8,128)S(1)} %convolution_add_fusion.19, bf16[1,512,512]{2,1,0:T(8,128)(2,1)S(1)} %copy-done.27, f32[512]{0:T(512)S(1)} %bitcast.281, ...), kind=kOutput, calls=%fused_computation.233.clone.1 | convolution fusion | flops 271581184 | bytes 5259264 | tf_op jit(solution)/shard_map/while/body/eval_jaxpr/dot_general | solution.py:108
  86.2 4.0 %fusion.208 = f32[1,512]{1,0:T(1,128)S(1)} fusion(f32[512,1]{0,1:T(1,128)S(1)} %reshape.662, f32[512,512]{1,0:T(8,128)S(1)} %get-tuple-element.679), kind=kOutput, calls=%fused_computation.17.clone.1 | convolution fusion | flops 3145728 | bytes 1052672 | tf_op jit(solution)/shard_map/while/body/eval_jaxpr/dot_general | solution.py:112
  90.2 4.1 %fusion.207 = f32[1,512,512]{2,1,0:T(8,128)S(1)} fusion(bf16[512,512]{1,0:T(8,128)(2,1)S(1)} %get-tuple-element.673, f32[1,512,512]{2,1,0:T(8,128)S(1)} %copy-done.4, pred[]{:T(512)S(6)} %compare.35, f32[512,1024]{1,0:T(8,128)S(1)} %convolution_add_fusion.19, f32[512]{0:T(512)S(1)} %bitcast.282, f32[512]{0:T(512)S(1)} %sub.107, ...), kind=kOutput, calls=%fused_computation.11.clone.1 | convolution fusion | flops 271056896 | bytes 3682305 | tf_op jit(solution)/shard_map/while/body/eval_jaxpr/dot_general | solution.py:121
  94.3 3.8 %fusion.205 = (bf16[512,512]{1,0:T(8,128)(2,1)S(1)}, f32[512,512]{1,0:T(8,128)S(1)}) fusion(f32[512,1024]{1,0:T(8,128)S(1)} %convolution_add_fusion.19, f32[512]{0:T(512)S(1)} %bitcast.283, f32[512]{0:T(512)S(1)} %sub.107, f32[512]{0:T(512)S(1)} %bitcast.286, f32[512]{0:T(512)S(1)} %get-tuple-element.670, f32[512]{0:T(512)S(1)} %bitcast.280, ...), kind=kOutput, calls=%fused_computation.235.clone.1 | convolution fusion | flops 270794752 | bytes 3682304 | tf_op jit(solution)/shard_map/while/body/eval_jaxpr/dot_general | solution.py:126
  100.5 1.5 fusion.211
  106.5 7.2 %fusion.204 = (bf16[512,512]{1,0:T(8,128)(2,1)S(1)}, f32[512,512]{1,0:T(8,128)S(1)}, f32[512,512]{1,0:T(8,128)S(1)}) fusion(f32[512]{0:T(512)S(1)} %copy-done.28, f32[512]{0:T(512)S(1)} %mul.582, f32[512,1024]{1,0:T(8,128)S(1)} %convolution_add_fusion.19, bf16[1,512,512]{2,1,0:T(8,128)(2,1)S(1)} %copy-done.27, f32[512]{0:T(512)S(1)} %bitcast.281, ...), kind=kOutput, calls=%fused_computation.233.clone.1 | convolution fusion | flops 271581184 | bytes 5259264 | tf_op jit(solution)/shard_map/while/body/eval_jaxpr/dot_general | solution.py:108
  113.7 4.0 %fusion.208 = f32[1,512]{1,0:T(1,128)S(1)} fusion(f32[512,1]{0,1:T(1,128)S(1)} %reshape.662, f32[512,512]{1,0:T(8,128)S(1)} %get-tuple-element.679), kind=kOutput, calls=%fused_computation.17.clone.1 | convolution fusion | flops 3145728 | bytes 1052672 | tf_op jit(solution)/shard_map/while/body/eval_jaxpr/dot_general | solution.py:112
  117.7 4.1 %fusion.207 = f32[1,512,512]{2,1,0:T(8,128)S(1)} fusion(bf16[512,512]{1,0:T(8,128)(2,1)S(1)} %get-tuple-element.673, f32[1,512,512]{2,1,0:T(8,128)S(1)} %copy-done.4, pred[]{:T(512)S(6)} %compare.35, f32[512,1024]{1,0:T(8,128)S(1)} %convolution_add_fusion.19, f32[512]{0:T(512)S(1)} %bitcast.282, f32[512]{0:T(512)S(1)} %sub.107, ...), kind=kOutput, calls=%fused_computation.11.clone.1 | convolution fusion | flops 271056896 | bytes 3682305 | tf_op jit(solution)/shard_map/while/body/eval_jaxpr/dot_general | solution.py:121
  121.8 3.8 %fusion.205 = (bf16[512,512]{1,0:T(8,128)(2,1)S(1)}, f32[512,512]{1,0:T(8,128)S(1)}) fusion(f32[512,1024]{1,0:T(8,128)S(1)} %convolution_add_fusion.19, f32[512]{0:T(512)S(1)} %bitcast.283, f32[512]{0:T(512)S(1)} %sub.107, f32[512]{0:T(512)S(1)} %bitcast.286, f32[512]{0:T(512)S(1)} %get-tuple-element.670, f32[512]{0:T(512)S(1)} %bitcast.280, ...), kind=kOutput, calls=%fused_computation.235.clone.1 | convolution fusion | flops 270794752 | bytes 3682304 | tf_op jit(solution)/shard_map/while/body/eval_jaxpr/dot_general | solution.py:126
  134.0 7.2 %fusion.204 = (bf16[512,512]{1,0:T(8,128)(2,1)S(1)}, f32[512,512]{1,0:T(8,128)S(1)}, f32[512,512]{1,0:T(8,128)S(1)}) fusion(f32[512]{0:T(512)S(1)} %copy-done.28, f32[512]{0:T(512)S(1)} %mul.582, f32[512,1024]{1,0:T(8,128)S(1)} %convolution_add_fusion.19, bf16[1,512,512]{2,1,0:T(8,128)(2,1)S(1)} %copy-done.27, f32[512]{0:T(512)S(1)} %bitcast.281, ...), kind=kOutput, calls=%fused_computation.233.clone.1 | convolution fusion | flops 271581184 | bytes 5259264 | tf_op jit(solution)/shard_map/while/body/eval_jaxpr/dot_general | solution.py:108
  141.1 4.0 %fusion.208 = f32[1,512]{1,0:T(1,128)S(1)} fusion(f32[512,1]{0,1:T(1,128)S(1)} %reshape.662, f32[512,512]{1,0:T(8,128)S(1)} %get-tuple-element.679), kind=kOutput, calls=%fused_computation.17.clone.1 | convolution fusion | flops 3145728 | bytes 1052672 | tf_op jit(solution)/shard_map/while/body/eval_jaxpr/dot_general | solution.py:112
  145.2 4.1 %fusion.207 = f32[1,512,512]{2,1,0:T(8,128)S(1)} fusion(bf16[512,512]{1,0:T(8,128)(2,1)S(1)} %get-tuple-element.673, f32[1,512,512]{2,1,0:T(8,128)S(1)} %copy-done.4, pred[]{:T(512)S(6)} %compare.35, f32[512,1024]{1,0:T(8,128)S(1)} %convolution_add_fusion.19, f32[512]{0:T(512)S(1)} %bitcast.282, f32[512]{0:T(512)S(1)} %sub.107, ...), kind=kOutput, calls=%fused_computation.11.clone.1 | convolution fusion | flops 271056896 | bytes 3682305 | tf_op jit(solution)/shard_map/while/body/eval_jaxpr/dot_general | solution.py:121
  149.3 3.8 %fusion.205 = (bf16[512,512]{1,0:T(8,128)(2,1)S(1)}, f32[512,512]{1,0:T(8,128)S(1)}) fusion(f32[512,1024]{1,0:T(8,128)S(1)} %convolution_add_fusion.19, f32[512]{0:T(512)S(1)} %bitcast.283, f32[512]{0:T(512)S(1)} %sub.107, f32[512]{0:T(512)S(1)} %bitcast.286, f32[512]{0:T(512)S(1)} %get-tuple-element.670, f32[512]{0:T(512)S(1)} %bitcast.280, ...), kind=kOutput, calls=%fused_computation.235.clone.1 | convolution fusion | flops 270794752 | bytes 3682304 | tf_op jit(solution)/shard_map/while/body/eval_jaxpr/dot_general | solution.py:126
  157.0 5.0 %copy.33 = f32[4,8,128,256]{3,1,2,0:T(8,128)S(1)} copy(f32[4,8,128,256]{3,2,1,0:T(8,128)} %get-tuple-element.323) | data formatting | bytes 8388608
  164.4 38.4 %all-reduce = (f32[1024]{0:T(1024)S(1)}, f32[3,512]{1,0:T(4,128)S(1)}, f32[512]{0:T(512)S(1)}) all-reduce(f32[1024]{0:T(1024)S(1)} %get-tuple-element.325, f32[3,512]{1,0:T(4,128)S(1)} %copy-done.18, f32[512]{0:T(512)S(1)} %copy-done.22), channel_id=1, replica_groups=mesh['lat'=4,'lon'=8] {'lat','lon'}, use_global_device_ids=true, to_apply=%region_7.8 | all-reduce | flops 3072 | bytes 24576 | tf_op jit(solution)/shard_map/psum | solution.py:288
  213.2 2.3 collective-permute-start.5
  217.0 2.6 collective-permute-start.7
  224.0 142.8 %all-reduce.4.cloned.1.call-done = (f32[9,256,256]{2,1,0:T(8,128)}, f32[256,1024]{1,0:T(8,128)}, f32[1,512,512]{2,1,0:T(8,128)}) async-done(((f32[9,256,256]{2,1,0:T(8,128)}, f32[256,1024]{1,0:T(8,128)}, f32[1,512,512]{2,1,0:T(8,128)}), (f32[9,256,256]{2,1,0:T(8,128)}, f32[256,1024]{1,0:T(8,128)}, f32[1,512,512]{2,1,0:T(8,128)})) %all-reduce.4.cloned.1.call-update) | async-done | bytes 4456464 | tf_op jit(solution)/shard_map/psum | solution.py:288
  366.8 3.4 broadcast_multiply_fusion
  (358 shorter events, 63.5 us)
Async XLA Ops:
  7.2 23.9 %copy-start.2 = (bf16[9,256,256]{2,1,0:T(8,128)(2,1)S(1)}, bf16[9,256,256]{2,1,0:T(8,128)(2,1)}, u32[]{:S(2)}) copy-start(bf16[9,256,256]{2,1,0:T(8,128)(2,1)} %param.14) | copy-start | bytes 3538948
  8.0 17.2 %collective-permute-start.1 = (bf16[1,16,256]{2,1,0:T(8,128)(2,1)S(1)}, bf16[1,16,256]{2,1,0:T(8,128)(2,1)S(1)}, u32[]{:S(2)}, u32[]{:S(2)}) collective-permute-start(bf16[1,16,256]{2,1,0:T(8,128)(2,1)S(1)} %get-tuple-element.522), channel_id=1, source_target_pairs={{8,0},{16,8},{24,16},{0,24},{9,1},{17,9},{25,17},{1,25},{10,2},{18... | collective-permute-start | bytes 24584 | tf_op jit(solution)/shard_map/ppermute | solution.py:23
  13.1 11.2 %collective-permute-start = (bf16[1,16,256]{2,1,0:T(8,128)(2,1)S(1)}, bf16[1,16,256]{2,1,0:T(8,128)(2,1)S(1)}, u32[]{:S(2)}, u32[]{:S(2)}) collective-permute-start(bf16[1,16,256]{2,1,0:T(8,128)(2,1)S(1)} %get-tuple-element.523), channel_id=1, source_target_pairs={{0,8},{8,16},{16,24},{24,0},{1,9},{9,17},{17,25},{25,1},{2,10},{10... | collective-permute-start | bytes 24584 | tf_op jit(solution)/shard_map/ppermute | solution.py:20
  16.9 18.1 %all-to-all-start = ((s32[32,1,192]{2,1,0:T(1,128)}), s32[32,1,192]{2,1,0:T(1,128)}, u32[]{:S(2)}, u32[]{:S(2)}) async-start(s32[32,1,192]{2,1,0:T(1,128)} %reshape.659), calls=%async_computation | async-start | bytes 65536 | tf_op jit(solution)/shard_map/all_to_all | solution.py:258
  25.2 5.5 %collective-permute-start.2 = (bf16[18,1,256]{2,1,0:T(2,128)(2,1)S(1)}, bf16[18,1,256]{2,1,0:T(2,128)(2,1)S(1)}, u32[]{:S(2)}, u32[]{:S(2)}) collective-permute-start(bf16[18,1,256]{2,1,0:T(2,128)(2,1)S(1)} %get-tuple-element.518), channel_id=1, source_target_pairs={{0,1},{1,2},{2,3},{3,4},{4,5},{5,6},{6,7},{7,0},{8,9},{9,10},{10,1... | collective-permute-start | bytes 27656 | tf_op jit(solution)/shard_map/ppermute | solution.py:20
  25.5 5.3 %collective-permute-start.3 = (bf16[18,1,256]{2,1,0:T(2,128)(2,1)S(1)}, bf16[18,1,256]{2,1,0:T(2,128)(2,1)S(1)}, u32[]{:S(2)}, u32[]{:S(2)}) collective-permute-start(bf16[18,1,256]{2,1,0:T(2,128)(2,1)S(1)} %get-tuple-element.519), channel_id=1, source_target_pairs={{1,0},{2,1},{3,2},{4,3},{5,4},{6,5},{7,6},{0,7},{9,8},{10,9},{11,1... | collective-permute-start | bytes 27656 | tf_op jit(solution)/shard_map/ppermute | solution.py:23
  32.4 14.6 %copy-start.1 = (bf16[256,1024]{1,0:T(8,128)(2,1)S(1)}, bf16[256,1024]{1,0:T(8,128)(2,1)}, u32[]{:S(2)}) copy-start(bf16[256,1024]{1,0:T(8,128)(2,1)} %param.15) | copy-start | bytes 1572868
  34.9 12.0 %all-to-all-start.1 = ((f32[32,1,64]{2,1,0:T(1,128)}), f32[32,1,64]{2,1,0:T(1,128)S(1)}, u32[]{:S(2)}, u32[]{:S(2)}) async-start(f32[32,1,64]{2,1,0:T(1,128)} %bitcast.22), calls=%async_computation.1 | async-start | bytes 32768 | tf_op jit(solution)/shard_map/all_to_all | solution.py:259
  39.8 327.0 %all-reduce.4.cloned.1.call-start = ((), (), s32[]{:S(2)}) async-start(), calls=%async_computation.2 | async-start | bytes 8912896 | tf_op jit(solution)/shard_map/psum | solution.py:288
  51.4 11.1 %copy-start.20 = (f32[512]{0:T(512)S(1)}, f32[512]{0:T(512)}, u32[]{:S(2)}) copy-start(f32[512]{0:T(512)} %get-tuple-element.706) | copy-start | bytes 6148 | tf_op jit(solution)/shard_map/while
  51.4 11.2 %copy-start.4 = (f32[1,512,512]{2,1,0:T(8,128)S(1)}, f32[1,512,512]{2,1,0:T(8,128)}, u32[]{:S(2)}) copy-start(f32[1,512,512]{2,1,0:T(8,128)} %get-tuple-element.705) | copy-start | bytes 3145732 | tf_op jit(solution)/shard_map/while
  62.7 4.1 %copy-start.21 = (f32[512]{0:T(512)}, f32[512]{0:T(512)S(1)}, u32[]{:S(2)}) copy-start(f32[512]{0:T(512)S(1)} %select_add_fusion.5) | copy-start | bytes 6148 | tf_op jit(solution)/shard_map/while
  66.8 4.0 %copy-start.16 = (f32[3,512]{1,0:T(4,128)S(1)}, f32[3,512]{1,0:T(4,128)}, u32[]{:S(2)}) copy-start(f32[3,512]{1,0:T(4,128)} %get-tuple-element.704) | copy-start | bytes 18436 | tf_op jit(solution)/shard_map/while
  79.0 11.1 %copy-start.20 = (f32[512]{0:T(512)S(1)}, f32[512]{0:T(512)}, u32[]{:S(2)}) copy-start(f32[512]{0:T(512)} %get-tuple-element.706) | copy-start | bytes 6148 | tf_op jit(solution)/shard_map/while
  79.0 11.2 %copy-start.4 = (f32[1,512,512]{2,1,0:T(8,128)S(1)}, f32[1,512,512]{2,1,0:T(8,128)}, u32[]{:S(2)}) copy-start(f32[1,512,512]{2,1,0:T(8,128)} %get-tuple-element.705) | copy-start | bytes 3145732 | tf_op jit(solution)/shard_map/while
  90.2 4.1 %copy-start.21 = (f32[512]{0:T(512)}, f32[512]{0:T(512)S(1)}, u32[]{:S(2)}) copy-start(f32[512]{0:T(512)S(1)} %select_add_fusion.5) | copy-start | bytes 6148 | tf_op jit(solution)/shard_map/while
  94.3 4.0 %copy-start.16 = (f32[3,512]{1,0:T(4,128)S(1)}, f32[3,512]{1,0:T(4,128)}, u32[]{:S(2)}) copy-start(f32[3,512]{1,0:T(4,128)} %get-tuple-element.704) | copy-start | bytes 18436 | tf_op jit(solution)/shard_map/while
  106.5 11.1 %copy-start.20 = (f32[512]{0:T(512)S(1)}, f32[512]{0:T(512)}, u32[]{:S(2)}) copy-start(f32[512]{0:T(512)} %get-tuple-element.706) | copy-start | bytes 6148 | tf_op jit(solution)/shard_map/while
  106.5 11.2 %copy-start.4 = (f32[1,512,512]{2,1,0:T(8,128)S(1)}, f32[1,512,512]{2,1,0:T(8,128)}, u32[]{:S(2)}) copy-start(f32[1,512,512]{2,1,0:T(8,128)} %get-tuple-element.705) | copy-start | bytes 3145732 | tf_op jit(solution)/shard_map/while
  117.7 4.1 %copy-start.21 = (f32[512]{0:T(512)}, f32[512]{0:T(512)S(1)}, u32[]{:S(2)}) copy-start(f32[512]{0:T(512)S(1)} %select_add_fusion.5) | copy-start | bytes 6148 | tf_op jit(solution)/shard_map/while
  121.8 4.0 %copy-start.16 = (f32[3,512]{1,0:T(4,128)S(1)}, f32[3,512]{1,0:T(4,128)}, u32[]{:S(2)}) copy-start(f32[3,512]{1,0:T(4,128)} %get-tuple-element.704) | copy-start | bytes 18436 | tf_op jit(solution)/shard_map/while
  134.0 11.1 %copy-start.20 = (f32[512]{0:T(512)S(1)}, f32[512]{0:T(512)}, u32[]{:S(2)}) copy-start(f32[512]{0:T(512)} %get-tuple-element.706) | copy-start | bytes 6148 | tf_op jit(solution)/shard_map/while
  134.0 11.2 %copy-start.4 = (f32[1,512,512]{2,1,0:T(8,128)S(1)}, f32[1,512,512]{2,1,0:T(8,128)}, u32[]{:S(2)}) copy-start(f32[1,512,512]{2,1,0:T(8,128)} %get-tuple-element.705) | copy-start | bytes 3145732 | tf_op jit(solution)/shard_map/while
  145.2 4.1 %copy-start.21 = (f32[512]{0:T(512)}, f32[512]{0:T(512)S(1)}, u32[]{:S(2)}) copy-start(f32[512]{0:T(512)S(1)} %select_add_fusion.5) | copy-start | bytes 6148 | tf_op jit(solution)/shard_map/while
  149.3 4.0 %copy-start.16 = (f32[3,512]{1,0:T(4,128)S(1)}, f32[3,512]{1,0:T(4,128)}, u32[]{:S(2)}) copy-start(f32[3,512]{1,0:T(4,128)} %get-tuple-element.704) | copy-start | bytes 18436 | tf_op jit(solution)/shard_map/while
  157.0 5.0 %copy-start = (f32[256,1024]{1,0:T(8,128)}, f32[256,1024]{1,0:T(8,128)S(1)}, u32[]{:S(2)}) copy-start(f32[256,1024]{1,0:T(8,128)S(1)} %get-tuple-element.324) | copy-start | bytes 3145732
  157.0 5.0 %copy-start.26 = (s32[1,32]{1,0:T(1,128)S(1)}, s32[1,32]{1,0:T(1,128)}, u32[]{:S(2)}) copy-start(s32[1,32]{1,0:T(1,128)} %param.21) | copy-start | bytes 388
  163.1 42.0 %copy-start.9 = (bf16[16,16,256]{2,1,0:T(8,128)(2,1)S(1)}, bf16[16,16,256]{2,1,0:T(8,128)(2,1)}, u32[]{:S(2)}) copy-start(bf16[16,16,256]{2,1,0:T(8,128)(2,1)} %copy-done.8) | copy-start | bytes 393220
  203.4 12.1 %collective-permute-start.4 = (bf16[1,16,256]{2,1,0:T(8,128)(2,1)S(1)}, bf16[1,16,256]{2,1,0:T(8,128)(2,1)S(1)}, u32[]{:S(2)}, u32[]{:S(2)}) collective-permute-start(bf16[1,16,256]{2,1,0:T(8,128)(2,1)S(1)} %get-tuple-element.521), channel_id=1, source_target_pairs={{0,8},{8,16},{16,24},{24,0},{1,9},{9,17},{17,25},{25,1},{2,10},{10... | collective-permute-start | bytes 24584 | tf_op jit(solution)/shard_map/ppermute | solution.py:20
  213.2 3.7 collective-permute-start.5
  216.9 4.1 %collective-permute-start.6 = (bf16[18,1,256]{2,1,0:T(2,128)(2,1)S(1)}, bf16[18,1,256]{2,1,0:T(2,128)(2,1)S(1)}, u32[]{:S(2)}, u32[]{:S(2)}) collective-permute-start(bf16[18,1,256]{2,1,0:T(2,128)(2,1)S(1)} %get-tuple-element.514), channel_id=1, source_target_pairs={{0,1},{1,2},{2,3},{3,4},{4,5},{5,6},{6,7},{7,0},{8,9},{9,10},{10,1... | collective-permute-start | bytes 27656 | tf_op jit(solution)/shard_map/ppermute | solution.py:20
  217.0 4.1 %collective-permute-start.7 = (bf16[18,1,256]{2,1,0:T(2,128)(2,1)S(1)}, bf16[18,1,256]{2,1,0:T(2,128)(2,1)S(1)}, u32[]{:S(2)}, u32[]{:S(2)}) collective-permute-start(bf16[18,1,256]{2,1,0:T(2,128)(2,1)S(1)} %get-tuple-element.515), channel_id=1, source_target_pairs={{1,0},{2,1},{3,2},{4,3},{5,4},{6,5},{7,6},{0,7},{9,8},{10,9},{11,1... | collective-permute-start | bytes 27656 | tf_op jit(solution)/shard_map/ppermute | solution.py:23
  (41 other events, 80.1 us)
Sparse Core Ops, SparseCore 0:
  220.4 146.3 all-reduce.3
where the time goes:
time: 381 us; the launch traced here: 380 us
  waiting for transfers between devices  150 us (39%)
  matrix products  110 us (29%)
  blocking collectives  38.4 us (10%)
  local copies, waits for them, and re-layouts  28.1 us (7%)
  starting transfers between devices  25.4 us (7%)
  between operations  14.6 us (4%)
  other arithmetic  12 us (3%)
    psum x1, waiting for transfers between devices, on_device(): lax.psum((conv_local, grad_totals[0], grad_totals[1], grad_totals[2], gra...  143 us
    psum x1, blocking collectives, on_device(): lax.psum((conv_local, grad_totals[0], grad_totals[1], grad_totals[2], gra...  38.4 us
    dot_general x4, matrix products, sine_grads(): jnp.dot(previous, hidden_weight[layer_index - 1], preferred_element_type=...  28.7 us
    dot_general x4, matrix products, sine_grads(): jnp.dot(inputs_rounded[layer_index - 1].T, rounded_grads[layer_index], pr...  16.2 us
    dot_general x4, matrix products, sine_grads(): output_grad = jnp.dot(cotan_rows, last_act, precision=lax.Precision.HIGHEST)  15.8 us
    dot_general x4, matrix products, sine_grads(): jnp.dot(rounded_grads[layer_index], hidden_weight[layer_index - 1].T, pre...  15.3 us
    ppermute x4, starting transfers between devices, padded_2(): lax.ppermute(lax.slice_in_dim(block, 0, width, axis=dim), axis, backward)  12.5 us
    dot_general x9, matrix products, conv_weight_grad(): jnp.dot(window.T, flat_grads, preferred_element_type=jnp.float32)  8.39 us
  transfers between devices with their start and end apart: 11, of which 4 were waited for; matrix products, arithmetic and copies ran while one was open for 7% of the time, Pallas kernels for 0%

commit v1 on v0

v1 whole, which is shorter than its diff:
```python
import functools

import jax
import jax.numpy as jnp
from jax import lax
from jax.experimental import pallas as pl
from jax.experimental.pallas import tpu as pltpu
from jax.sharding import PartitionSpec as P

BLOCK = 128
LEVELS = 37
SUB = 6


OMEGA = 30.0
TILE = 512


def padded_2(block, sides, width):
    for axis, dim in sides:
        count = lax.axis_size(axis)
        forward = [(i, i + 1) for i in range(count - 1)]
        forward.append((count - 1, 0))
        backward = [(target, source) for source, target in forward]
        low = lax.ppermute(
            lax.slice_in_dim(block, block.shape[dim] - width, None, axis=dim), axis, forward
        )
        high = lax.ppermute(lax.slice_in_dim(block, 0, width, axis=dim), axis, backward)
        block = jnp.concatenate([low, block, high], axis=dim)
    return block


def conv_apply(padded, kernel, row_count, col_count, flipped):
    channels = padded.shape[-1]
    result = jnp.zeros((row_count * col_count, kernel.shape[-1]), jnp.float32)
    for shift_a in (-1, 0, 1):
        for shift_b in (-1, 0, 1):
            tap_index = (shift_a + 1) * 3 + shift_b + 1
            if flipped:
                window = padded[
                    1 - shift_a : 1 - shift_a + row_count, 1 - shift_b : 1 - shift_b + col_count
                ]
                matrix = kernel[tap_index].T
            else:
                window = padded[
                    1 + shift_a : 1 + shift_a + row_count, 1 + shift_b : 1 + shift_b + col_count
                ]
                matrix = kernel[tap_index]
            result = result + jnp.dot(
                window.reshape(row_count * col_count, channels),
                matrix,
                preferred_element_type=jnp.float32,
            )
    return result


def conv_weight_grad(padded, grads, row_count, col_count):
    flat_grads = grads.reshape(row_count * col_count, -1)
    pieces = []
    for shift_a in (-1, 0, 1):
        for shift_b in (-1, 0, 1):
            window = padded[
                1 + shift_a : 1 + shift_a + row_count, 1 + shift_b : 1 + shift_b + col_count
            ]
            window = window.reshape(row_count * col_count, -1)
            pieces.append(jnp.dot(window.T, flat_grads, preferred_element_type=jnp.float32))
    return jnp.stack(pieces)


def close_poles(padded, lat_pos, lat_parts):
    top_rim = jnp.where(lat_pos == 0, jnp.zeros_like(padded[:1]), padded[:1])
    bottom_rim = jnp.where(lat_pos == lat_parts - 1, jnp.zeros_like(padded[-1:]), padded[-1:])
    return jnp.concatenate([top_rim, padded[1:-1], bottom_rim], axis=0)


SIN_TERMS = (
    0.7071067781421408,
    -0.029462767114633488,
    0.0003682722504284759,
    -2.1886040931894034e-06,
    7.195418014521965e-09,
)
COS_TERMS = (
    1.4142134959273227,
    -0.17677635831469551,
    0.0036825740917005817,
    -3.061241565438332e-05,
    1.2789559619534725e-07,
)
TURN = 6.283185307179586
TURN_HIGH = 6.28125
TURN_LOW = TURN - TURN_HIGH
EXTRA = 16
COORD_ROWS = 32
CHUNK = 64
LANES = 128


def sin_cos(angle):
    turns = jnp.round(angle * (1.0 / TURN))
    rest = (angle - turns * TURN_HIGH) - turns * TURN_LOW
    square = rest * rest

    def series(terms):
        value = jnp.full_like(square, terms[-1])
        for term in terms[-2::-1]:
            value = value * square + term
        return value

    half_sin = rest * series(SIN_TERMS)
    half_cos = series(COS_TERMS)
    return half_sin * half_cos, 1.0 - half_sin * half_sin


def query_kernel(
    cuts,
    scale,
    offsets_ref,
    rows_ref,
    coords_ref,
    features_ref,
    map_ref,
    coord_weight_ref,
    columns_ref,
    hidden_ref,
    map_grad_ref,
    hidden_grad_ref,
    small_ref,
    feature_grad_ref,
    feat_t,
    weight0,
    weight1,
    column_tiles,
    stack0,
    stack1,
    picks,
    pre,
    cos0,
    rounded0,
    rounded1,
    sums,
    hidden_sums,
    out_sums,
):
    step = pl.program_id(0)
    cells, channels = features_ref.shape
    hidden = hidden_ref.shape[0]
    block = rows_ref.shape[1]
    f32, bf16 = jnp.float32, jnp.bfloat16

    @pl.when(step == 0)
    def _():
        feat_t[...] = features_ref[...].T
        weight0[:, :channels] = map_ref[:, :hidden].T
        coef = coord_weight_ref[...]
        high = coef.astype(bf16).astype(f32)
        mid = (coef - high).astype(bf16).astype(f32)
        low = coef - high - mid
        parts = jnp.concatenate([high, mid, low, jnp.zeros((LANES - 24, hidden), f32)], axis=0)
        weight0[:, channels:] = parts.T.astype(bf16)
        weight1[:, :hidden] = hidden_ref[...].T
        weight1[:, hidden:] = map_ref[:, hidden:].T
        column_tiles[...] = columns_ref[...].T
        stack0[...] = jnp.zeros_like(stack0)
        sums[...] = jnp.zeros_like(sums)
        hidden_sums[...] = jnp.zeros_like(hidden_sums)
        out_sums[...] = jnp.zeros_like(out_sums)

    cell = rows_ref[0:1, :].astype(jnp.int32)
    ids = lax.broadcasted_iota(jnp.int32, (cells, block), 0)
    picks[:cells, :] = jnp.where(ids == cell, 1.0, 0.0).astype(bf16)
    picks[cells:, :] = coords_ref[:EXTRA, :]
    queried = jnp.dot(feat_t[...], picks[:cells, :], preferred_element_type=f32).astype(bf16)
    stack0[:channels, :] = queried
    stack0[channels : channels + COORD_ROWS, :] = coords_ref[...]
    stack1[hidden:, :] = queried
    pre[...] = jnp.dot(weight0[...], stack0[...], preferred_element_type=f32)
    for top in range(0, hidden, CHUNK):
        for left in range(0, block, LANES):
            at = (slice(top, top + CHUNK), slice(left, left + LANES))
            sine, cosine = sin_cos(pre[at])
            stack1[at] = sine.astype(bf16)
            cos0[at] = cosine
    pre[...] = jnp.dot(weight1[...], stack1[...], preferred_element_type=f32)
    for top in range(0, hidden, CHUNK):
        rows = slice(top, top + CHUNK)
        bias = column_tiles[rows, :LANES]
        out_weight = column_tiles[rows, LANES:]
        total = out_sums[rows, :]
        for left in range(0, block, LANES):
            at = (rows, slice(left, left + LANES))
            cotan = rows_ref[1:2, left : left + LANES]
            sine, cosine = sin_cos(pre[at] + bias)
            total = total + sine * cotan
            rounded1[at] = (out_weight * cotan * cosine).astype(bf16)
        out_sums[rows, :] = total
    act_grad = jnp.dot(hidden_ref[...], rounded1[...], preferred_element_type=f32)
    rounded0[...] = (act_grad * cos0[...]).astype(bf16)
    across = (((1,), (1,)), ((), ()))
    sums[:, hidden:] += lax.dot_general(
        picks[...], rounded1[...], across, preferred_element_type=f32
    )
    hidden_sums[...] += lax.dot_general(
        stack1[:hidden, :], rounded1[...], across, preferred_element_type=f32
    )
    sums[:, :hidden] += lax.dot_general(
        picks[...], rounded0[...], across, preferred_element_type=f32
    )

    @pl.when(step == pl.num_programs(0) - 1)
    def _():
        cell_sums = sums[:cells, :]
        upper = cell_sums.astype(bf16)
        lower = (cell_sums - upper.astype(f32)).astype(bf16)
        map_grad_ref[...] = (
            jnp.dot(feat_t[...], upper, preferred_element_type=f32)
            + jnp.dot(feat_t[...], lower, preferred_element_type=f32)
        ) * scale
        feature_grad_ref[...] = (
            lax.dot_general(upper, map_ref[...], across, preferred_element_type=f32)
            + lax.dot_general(lower, map_ref[...], across, preferred_element_type=f32)
        ).astype(bf16)
        hidden_grad_ref[...] = hidden_sums[...] * scale
        extra = sums[cells : cells + 8, :]
        lat_cell, lat_sub, lon_cell, lon_sub, level, level_offset = cuts
        total = extra[5:6, :hidden]
        lat_grad = (
            lat_cell * extra[0:1, :hidden]
            + lat_sub * extra[1:2, :hidden]
            + offsets_ref[0] * total
        )
        lon_grad = (
            lon_cell * extra[2:3, :hidden]
            + lon_sub * extra[3:4, :hidden]
            + offsets_ref[1] * total
        )
        level_grad = level * extra[4:5, :hidden] + level_offset * total
        out_grad = jnp.sum(out_sums[...].T, axis=0, keepdims=True)
        gain = OMEGA * scale
        small_ref[...] = jnp.zeros_like(small_ref)
        small_ref[0:1, :] = extra[5:6, :] * scale
        small_ref[1:2, :] = jnp.concatenate([lat_grad, lon_grad], axis=1) * gain
        small_ref[2:3, :] = jnp.concatenate([level_grad * gain, out_grad * scale], axis=1)


def query_pass(
    features, rows, coords, offsets, coord_weight, columns, map_weight, hidden_weight, cuts, scale
):
    cells, channels = features.shape
    queries = rows.shape[1]
    hidden = hidden_weight.shape[0]
    width = map_weight.shape[1]
    block = min(TILE, queries)
    f32, bf16 = jnp.float32, jnp.bfloat16

    def whole(shape):
        return pl.BlockSpec(shape, lambda i: (0,) * len(shape))

    return pl.pallas_call(
        functools.partial(query_kernel, cuts, scale),
        grid=(queries // block,),
        in_specs=[
            pl.BlockSpec(memory_space=pltpu.SMEM),
            pl.BlockSpec((rows.shape[0], block), lambda i: (0, i)),
            pl.BlockSpec((COORD_ROWS, block), lambda i: (0, i)),
            whole(features.shape),
            whole(map_weight.shape),
            whole(coord_weight.shape),
            whole(columns.shape),
            whole(hidden_weight.shape),
        ],
        out_specs=[
            whole((channels, width)),
            whole((hidden, hidden)),
            whole((8, width)),
            whole((cells, channels)),
        ],
        out_shape=[
            jax.ShapeDtypeStruct((channels, width), f32),
            jax.ShapeDtypeStruct((hidden, hidden), f32),
            jax.ShapeDtypeStruct((8, width), f32),
            jax.ShapeDtypeStruct((cells, channels), bf16),
        ],
        scratch_shapes=[
            pltpu.VMEM((channels, cells), bf16),
            pltpu.VMEM((hidden, channels + LANES), bf16),
            pltpu.VMEM((hidden, hidden + channels), bf16),
            pltpu.VMEM((hidden, 2 * LANES), f32),
            pltpu.VMEM((channels + LANES, block), bf16),
            pltpu.VMEM((hidden + channels, block), bf16),
            pltpu.VMEM((cells + EXTRA, block), bf16),
            pltpu.VMEM((hidden, block), f32),
            pltpu.VMEM((hidden, block), f32),
            pltpu.VMEM((hidden, block), bf16),
            pltpu.VMEM((hidden, block), bf16),
            pltpu.VMEM((cells + EXTRA, width), f32),
            pltpu.VMEM((hidden, hidden), f32),
            pltpu.VMEM((hidden, LANES), f32),
        ],
        compiler_params=pltpu.CompilerParams(vmem_limit_bytes=48 * 1024 * 1024),
        name="queries",
    )(offsets, rows, coords, features, map_weight, coord_weight, columns, hidden_weight)


def on_device(
    latents,
    conv_weight,
    map_weight,
    map_bias,
    input_weight,
    hidden_weight,
    output_weight,
    hit_owner,
    serve_block,
    query_grid,
    cotangent,
):
    lat_tile, lon_tile, channels = latents.shape
    lat_parts = lax.axis_size("lat")
    lon_parts = lax.axis_size("lon")
    dev_count = lat_parts * lon_parts
    lat_cells = lat_tile * lat_parts
    lon_cells = lon_tile * lon_parts
    block_rows = BLOCK
    lat_pos = lax.axis_index("lat")
    lon_pos = lax.axis_index("lon")
    padded = close_poles(padded_2(latents, (("lat", 0), ("lon", 1)), 1), lat_pos, lat_parts)
    features = conv_apply(padded, conv_weight, lat_tile, lon_tile, False).astype(jnp.bfloat16)
    serve_row = serve_block[0]
    hit_count = hit_owner.shape[0]
    group_size = cotangent.shape[0] // hit_count
    grid_groups = query_grid.reshape(3, hit_count, group_size).transpose(1, 0, 2)
    query_rows = jnp.concatenate(
        [
            grid_groups.astype(jnp.float32),
            cotangent.reshape(hit_count, 1, group_size),
        ],
        axis=1,
    ).reshape(hit_count, 4 * group_size)
    sent = jnp.zeros((dev_count, 4 * group_size), jnp.float32).at[hit_owner].set(query_rows)
    got = lax.all_to_all(sent, ("lat", "lon"), split_axis=0, concat_axis=0, tiled=True)
    got = got.reshape(dev_count, 4, group_size).transpose(1, 0, 2)
    block_cell = got[0].astype(jnp.int32)
    sub = got[1].astype(jnp.int32)
    tile_cell = jnp.where(
        serve_row[:, None] < 0, -1, serve_row[:, None] * block_rows + block_cell
    )
    queries = dev_count * group_size
    zero_row = jnp.zeros((dev_count, group_size), jnp.int32)
    coord_group = jnp.stack(
        [
            tile_cell // lon_tile,
            sub // SUB,
            tile_cell % lon_tile,
            sub % SUB,
            got[2].astype(jnp.int32),
            zero_row + 1,
            zero_row,
            zero_row,
        ]
    ).reshape(8, queries)
    coords = jnp.concatenate([coord_group] * 3 + [jnp.zeros_like(coord_group)], axis=0).astype(
        jnp.bfloat16
    )
    rows = jnp.concatenate(
        [tile_cell.astype(jnp.float32)[None], got[3][None]], axis=0
    ).reshape(2, queries)
    rows = jnp.pad(rows, ((0, 6), (0, 0)))
    lat_offset = (2 * SUB * lat_tile * lat_pos + 1).astype(jnp.float32) / (lat_cells * SUB) - 1.0
    lon_offset = (2 * SUB * lon_tile * lon_pos + 1).astype(jnp.float32) / (lon_cells * SUB) - 1.0
    level_offset = 1.0 / LEVELS - 1.0
    cuts = (
        2.0 / lat_cells,
        2.0 / (lat_cells * SUB),
        2.0 / lon_cells,
        2.0 / (lon_cells * SUB),
        2.0 / LEVELS,
        level_offset,
    )
    width = input_weight.shape[1]
    coord_weight = jnp.stack(
        [
            OMEGA * cuts[0] * input_weight[0],
            OMEGA * cuts[1] * input_weight[0],
            OMEGA * cuts[2] * input_weight[1],
            OMEGA * cuts[3] * input_weight[1],
            OMEGA * cuts[4] * input_weight[2],
            OMEGA
            * (
                lat_offset * input_weight[0]
                + lon_offset * input_weight[1]
                + level_offset * input_weight[2]
            )
            + map_bias[:width],
            jnp.zeros_like(input_weight[0]),
            jnp.zeros_like(input_weight[0]),
        ]
    )
    columns = jnp.concatenate(
        [
            jnp.broadcast_to(map_bias[None, width:], (LANES, width)),
            jnp.broadcast_to(output_weight[None, :], (LANES, width)),
        ],
        axis=0,
    )
    grad_scale = float(hit_count * group_size * dev_count) ** (-0.5)
    map_grad, hidden_grad, small, tile_grads = query_pass(
        features,
        rows,
        coords,
        jnp.stack([lat_offset, lon_offset]),
        coord_weight,
        columns,
        map_weight,
        hidden_weight[0],
        cuts,
        grad_scale,
    )
    feature_grad = tile_grads.reshape(lat_tile, lon_tile, channels).astype(jnp.bfloat16)
    padded_grad = close_poles(
        padded_2(feature_grad, (("lat", 0), ("lon", 1)), 1), lat_pos, lat_parts
    )
    latent_grad = conv_apply(padded_grad, conv_weight, lat_tile, lon_tile, True).reshape(
        lat_tile, lon_tile, channels
    )
    conv_local = conv_weight_grad(padded, feature_grad, lat_tile, lon_tile)
    conv_total, map_total, hidden_total, small_total = lax.psum(
        (conv_local * grad_scale, map_grad, hidden_grad, small), ("lat", "lon")
    )
    input_total = jnp.stack(
        [small_total[1, :width], small_total[1, width:], small_total[2, :width]]
    )
    return (
        latent_grad,
        conv_total,
        map_total,
        small_total[0],
        input_total,
        hidden_total[None],
        small_total[2, width:],
    )


def solution(mesh):
    placed = (
        P("lat", "lon", None),
        P(),
        P(),
        P(),
        P(),
        P(),
        P(),
        P(("lat", "lon")),
        P(("lat", "lon"), None),
        P(None, ("lat", "lon")),
        P(("lat", "lon")),
    )
    return jax.shard_map(
        on_device,
        mesh=mesh,
        in_specs=placed,
        out_specs=(P("lat", "lon", None), P(), P(), P(), P(), P(), P()),
        check_vma=False,
    )
```

time: 381 us -> 266 us (0.70)
  matrix products: 110 us -> 8.25 us
  Pallas kernels: 0 us -> 18.3 us
  local copies, waits for them, and re-layouts: 28.1 us -> 11.4 us
  starting transfers between devices: 25.4 us -> 18.7 us
  other arithmetic: 12 us -> 7.47 us
  waiting for transfers between devices: 150 us -> 146 us
    dot_general x47 -> x0, matrix products: 96.7 us -> none  [the longest x4 28.7 us: sine_grads(): jnp.dot(previous, hidden_weight[layer_index - 1], preferred_element_type=...]
    pallas_call x0 -> x1, Pallas kernels: none -> 18.3 us  [query_pass(): pl.pallas_call(functools.partial(query_kernel, cuts, scale), grid=(querie...]
    all_to_all x2 -> x1, starting transfers between devices: 11 us -> 4.27 us  [on_device(): lax.all_to_all(sent, ('lat', 'lon'), split_axis=0, concat_axis=0, tiled=T...]
    dot_general x9, matrix products: 8.39 us -> 2.93 us  [conv_weight_grad(): jnp.dot(window.T, flat_grads, preferred_element_type=jnp.float32)]
    all_to_all x2 -> x1, waiting for transfers between devices: 5 us -> 0.01 us  [on_device(): lax.all_to_all(sent, ('lat', 'lon'), split_axis=0, concat_axis=0, tiled=T...]
    dynamic_slice x4 -> x0, local copies, waits for them, and re-layouts: 4.32 us -> none  [run_groups(): grad_totals, block_grads = lax.scan(advance, initial, inputs)]
    mul x6 -> x3, other arithmetic: 7.33 us -> 3.1 us  [the longest x1 1.61 us: on_device(): conv_local * grad_scale]
  transfers between devices with their start and end apart: 11 -> 10, of which waited for: 4 -> 4; matrix products, arithmetic and copies ran while one was open for 7% -> 5% of each run, Pallas kernels for 0% -> 0%
where the time goes in v1:
time: 266 us; the launch traced here: 265 us
  waiting for transfers between devices  146 us (55%)
  blocking collectives  40.6 us (15%)
  starting transfers between devices  18.7 us (7%)
  Pallas kernels  18.3 us (7%)
  between operations  14.8 us (6%)
  local copies, waits for them, and re-layouts  11.4 us (4%)
  matrix products  8.25 us (3%)
  other arithmetic  7.47 us (3%)
    psum x1, waiting for transfers between devices, on_device(): lax.psum((conv_local * grad_scale, map_grad, hidden_grad, small), ('lat',...  143 us
    psum x1, blocking collectives, on_device(): lax.psum((conv_local * grad_scale, map_grad, hidden_grad, small), ('lat',...  40.6 us
    pallas_call x1, Pallas kernels, query_pass(): pl.pallas_call(functools.partial(query_kernel, cuts, scale), grid=(querie...  18.3 us
    ppermute x4, starting transfers between devices, padded_2(): lax.ppermute(lax.slice_in_dim(block, 0, width, axis=dim), axis, backward)  9.34 us
    unnamed x47, local copies, waits for them, and re-layouts  6.05 us
  transfers between devices with their start and end apart: 10, of which 4 were waited for; matrix products, arithmetic and copies ran while one was open for 5% of the time, Pallas kernels for 0%

profile of v1, /device:TPU:0, one launch (start us, length us, event | category | flops | bytes accessed | tf_op | source)
XLA Modules:
  0.0 265.1 jit_solution(4505462167525950930)
XLA Ops:
  7.2 0.7 fusion.75
  7.9 3.1 %collective-permute-start = (bf16[1,16,256]{2,1,0:T(8,128)(2,1)S(1)}, bf16[1,16,256]{2,1,0:T(8,128)(2,1)S(1)}, u32[]{:S(2)}, u32[]{:S(2)}) collective-permute-start(bf16[1,16,256]{2,1,0:T(8,128)(2,1)S(1)} %get-tuple-element.58), channel_id=1, source_target_pairs={{0,8},{8,16},{16,24},{24,0},{1,9},{9,17},{17,25},{25,1},{2,10},{10... | collective-permute-start | bytes 24584 | tf_op jit(solution)/shard_map/ppermute | solution.py:25
  11.0 2.0 collective-permute-start.1
  13.0 0.7 convert_element_type.42
  13.8 0.8 reshape.181
  14.8 0.7 compare_select_fusion.3
  15.5 0.7 scatter_custom_fusion
  16.2 0.6 all_to_all.6
  16.8 4.3 %all-to-all-start = ((f32[32,1,256]{2,1,0:T(1,128)}), f32[32,1,256]{2,1,0:T(1,128)S(1)}, u32[]{:S(2)}, u32[]{:S(2)}) async-start(f32[32,1,256]{2,1,0:T(1,128)} %all_to_all.6), calls=%async_computation | async-start | bytes 65536 | tf_op jit(solution)/shard_map/all_to_all | solution.py:341
  21.1 0.7 compare_bitcast_fusion
  21.8 0.7 multiply_bitcast_fusion
  22.4 1.1 fusion.34
  23.6 0.8 add_multiply_fusion
  25.0 2.4 collective-permute-start.3
  27.5 1.3 collective-permute-done.2
  32.9 18.3 %queries.1 = (f32[256,1024]{1,0:T(8,128)}, f32[512,512]{1,0:T(8,128)}, f32[8,1024]{1,0:T(8,128)S(1)}, bf16[256,256]{1,0:T(8,128)(2,1)S(1)}) custom-call(f32[2]{0:T(128)S(1)} %pad_maximum_fusion.20.offsets_ref, f32[8,2048]{1,0:T(8,128)S(1)} %select_maximum_fusion.rows_ref, bf16[32,2048]{1,0:T(8,128)(2,1)S(1)} %concatenate.70.coords_ref, ...), custom_call_target="tpu_custom_call" | custom-call | tf_op jit(solution)/shard_map/queries/pallas_call | solution.py:259
  51.2 1.2 fusion.12
  54.5 1.6 broadcast_multiply_fusion
  56.1 40.6 %psum.30 = f32[8,1024]{1,0:T(8,128)S(1)} all-reduce(f32[8,1024]{1,0:T(8,128)S(1)} %get-tuple-element.13), channel_id=1, replica_groups=mesh['lat'=4,'lon'=8] {'lat','lon'}, use_global_device_ids=true, to_apply=%region_3.4 | all-reduce | flops 8192 | bytes 65536 | tf_op jit(solution)/shard_map/psum | solution.py:427
  96.7 1.6 collective-permute-start.4
  98.3 2.3 collective-permute-start.5
  100.6 0.6 fusion.76
  101.2 1.0 collective-permute-done.4
  102.3 2.6 collective-permute-start.7
  105.0 0.6 pad_maximum_fusion.19
  105.6 0.6 slice.293
  108.4 0.9 convolution_add_fusion
  109.3 143.0 %all-reduce.4.cloned.1.call-done = (f32[9,256,256]{2,1,0:T(8,128)}, f32[256,1024]{1,0:T(8,128)}, f32[1,512,512]{2,1,0:T(8,128)}) async-done(((f32[9,256,256]{2,1,0:T(8,128)}, f32[256,1024]{1,0:T(8,128)}, f32[1,512,512]{2,1,0:T(8,128)}), (f32[9,256,256]{2,1,0:T(8,128)}, f32[256,1024]{1,0:T(8,128)}, f32[1,512,512]{2,1,0:T(8,128)})) %all-reduce.4.cloned.1.call-update) | async-done | bytes 4456464 | tf_op jit(solution)/shard_map/psum | solution.py:427
  252.3 3.3 %copy.41 = f32[9,256,256]{2,1,0:T(8,128)} copy(f32[9,256,256]{2,1,0:T(8,128)} %get-tuple-element.74) | data formatting | bytes 4718592
  255.7 1.0 copy.42
  256.6 0.6 copy-done.17
  257.3 1.0 copy.43
  (121 shorter events, 8.9 us)
Async XLA Ops:
  7.2 17.3 %copy-start.19 = (f32[1024]{0:T(1024)S(1)}, f32[1024]{0:T(1024)}, u32[]{:S(2)}) copy-start(f32[1024]{0:T(1024)} %param.14) | copy-start | bytes 12292
  7.2 17.3 %copy-start.20 = (f32[512]{0:T(512)S(1)}, f32[512]{0:T(512)}, u32[]{:S(2)}) copy-start(f32[512]{0:T(512)} %param.17) | copy-start | bytes 6148
  7.9 16.6 %collective-permute-start = (bf16[1,16,256]{2,1,0:T(8,128)(2,1)S(1)}, bf16[1,16,256]{2,1,0:T(8,128)(2,1)S(1)}, u32[]{:S(2)}, u32[]{:S(2)}) collective-permute-start(bf16[1,16,256]{2,1,0:T(8,128)(2,1)S(1)} %get-tuple-element.58), channel_id=1, source_target_pairs={{0,8},{8,16},{16,24},{24,0},{1,9},{9,17},{17,25},{25,1},{2,10},{10... | collective-permute-start | bytes 24584 | tf_op jit(solution)/shard_map/ppermute | solution.py:25
  11.0 13.7 %collective-permute-start.1 = (bf16[1,16,256]{2,1,0:T(8,128)(2,1)S(1)}, bf16[1,16,256]{2,1,0:T(8,128)(2,1)S(1)}, u32[]{:S(2)}, u32[]{:S(2)}) collective-permute-start(bf16[1,16,256]{2,1,0:T(8,128)(2,1)S(1)} %get-tuple-element.57), channel_id=1, source_target_pairs={{8,0},{16,8},{24,16},{0,24},{9,1},{17,9},{25,17},{1,25},{10,2},{18... | collective-permute-start | bytes 24584 | tf_op jit(solution)/shard_map/ppermute | solution.py:28
  14.8 9.8 %copy-start.3 = (bf16[16,16,256]{2,1,0:T(8,128)(2,1)S(1)}, bf16[16,16,256]{2,1,0:T(8,128)(2,1)}, u32[]{:S(2)}) copy-start(bf16[16,16,256]{2,1,0:T(8,128)(2,1)} %param.11) | copy-start | bytes 393220
  16.8 14.2 %all-to-all-start = ((f32[32,1,256]{2,1,0:T(1,128)}), f32[32,1,256]{2,1,0:T(1,128)S(1)}, u32[]{:S(2)}, u32[]{:S(2)}) async-start(f32[32,1,256]{2,1,0:T(1,128)} %all_to_all.6), calls=%async_computation | async-start | bytes 65536 | tf_op jit(solution)/shard_map/all_to_all | solution.py:341
  21.1 231.3 %all-reduce.4.cloned.1.call-start = ((), (), s32[]{:S(2)}) async-start(), calls=%async_computation.1 | async-start | bytes 8912896 | tf_op jit(solution)/shard_map/psum | solution.py:427
  24.6 4.6 %copy-start.2 = (bf16[9,256,256]{2,1,0:T(8,128)(2,1)S(1)}, bf16[9,256,256]{2,1,0:T(8,128)(2,1)}, u32[]{:S(2)}) copy-start(bf16[9,256,256]{2,1,0:T(8,128)(2,1)} %param.12) | copy-start | bytes 3538948
  24.7 4.1 %collective-permute-start.2 = (bf16[18,1,256]{2,1,0:T(2,128)(2,1)S(1)}, bf16[18,1,256]{2,1,0:T(2,128)(2,1)S(1)}, u32[]{:S(2)}, u32[]{:S(2)}) collective-permute-start(bf16[18,1,256]{2,1,0:T(2,128)(2,1)S(1)} %get-tuple-element.53), channel_id=1, source_target_pairs={{0,1},{1,2},{2,3},{3,4},{4,5},{5,6},{6,7},{7,0},{8,9},{9,10},{10,1... | collective-permute-start | bytes 27656 | tf_op jit(solution)/shard_map/ppermute | solution.py:25
  25.0 3.9 %collective-permute-start.3 = (bf16[18,1,256]{2,1,0:T(2,128)(2,1)S(1)}, bf16[18,1,256]{2,1,0:T(2,128)(2,1)S(1)}, u32[]{:S(2)}, u32[]{:S(2)}) collective-permute-start(bf16[18,1,256]{2,1,0:T(2,128)(2,1)S(1)} %get-tuple-element.54), channel_id=1, source_target_pairs={{1,0},{2,1},{3,2},{4,3},{5,4},{6,5},{7,6},{0,7},{9,8},{10,9},{11,1... | collective-permute-start | bytes 27656 | tf_op jit(solution)/shard_map/ppermute | solution.py:28
  29.1 0.8 copy-start.6
  29.1 0.8 copy-start.8
  29.1 0.8 copy-start.10
  29.1 0.8 copy-start.12
  29.1 1.4 copy-start.4
  30.1 0.7 copy-start.13
  30.1 0.7 copy-start.15
  30.5 2.4 copy-start
  30.5 2.4 copy-start.1
  32.9 19.7 %copy-start.11 = (bf16[16,16,256]{2,1,0:T(8,128)(2,1)S(1)}, bf16[16,16,256]{2,1,0:T(8,128)(2,1)}, u32[]{:S(2)}) copy-start(bf16[16,16,256]{2,1,0:T(8,128)(2,1)} %copy-done.10) | copy-start | bytes 393220
  51.2 1.7 copy-start.9
  51.2 1.9 copy-start.16
  52.6 1.0 copy-start.14
  52.9 1.0 copy-start.7
  53.1 0.9 copy-start.5
  96.7 5.5 %collective-permute-start.4 = (bf16[1,16,256]{2,1,0:T(8,128)(2,1)S(1)}, bf16[1,16,256]{2,1,0:T(8,128)(2,1)S(1)}, u32[]{:S(2)}, u32[]{:S(2)}) collective-permute-start(bf16[1,16,256]{2,1,0:T(8,128)(2,1)S(1)} %get-tuple-element.55), channel_id=1, source_target_pairs={{0,8},{8,16},{16,24},{24,0},{1,9},{9,17},{17,25},{25,1},{2,10},{10... | collective-permute-start | bytes 24584 | tf_op jit(solution)/shard_map/ppermute | solution.py:25
  98.3 3.9 %collective-permute-start.5 = (bf16[1,16,256]{2,1,0:T(8,128)(2,1)S(1)}, bf16[1,16,256]{2,1,0:T(8,128)(2,1)S(1)}, u32[]{:S(2)}, u32[]{:S(2)}) collective-permute-start(bf16[1,16,256]{2,1,0:T(8,128)(2,1)S(1)} %get-tuple-element.56), channel_id=1, source_target_pairs={{8,0},{16,8},{24,16},{0,24},{9,1},{17,9},{25,17},{1,25},{10,2},{18... | collective-permute-start | bytes 24584 | tf_op jit(solution)/shard_map/ppermute | solution.py:28
  102.3 4.1 %collective-permute-start.6 = (bf16[18,1,256]{2,1,0:T(2,128)(2,1)S(1)}, bf16[18,1,256]{2,1,0:T(2,128)(2,1)S(1)}, u32[]{:S(2)}, u32[]{:S(2)}) collective-permute-start(bf16[18,1,256]{2,1,0:T(2,128)(2,1)S(1)} %get-tuple-element.49), channel_id=1, source_target_pairs={{0,1},{1,2},{2,3},{3,4},{4,5},{5,6},{6,7},{7,0},{8,9},{9,10},{10,1... | collective-permute-start | bytes 27656 | tf_op jit(solution)/shard_map/ppermute | solution.py:25
  102.3 4.1 %collective-permute-start.7 = (bf16[18,1,256]{2,1,0:T(2,128)(2,1)S(1)}, bf16[18,1,256]{2,1,0:T(2,128)(2,1)S(1)}, u32[]{:S(2)}, u32[]{:S(2)}) collective-permute-start(bf16[18,1,256]{2,1,0:T(2,128)(2,1)S(1)} %get-tuple-element.50), channel_id=1, source_target_pairs={{1,0},{2,1},{3,2},{4,3},{5,4},{6,5},{7,6},{0,7},{9,8},{10,9},{11,1... | collective-permute-start | bytes 27656 | tf_op jit(solution)/shard_map/ppermute | solution.py:28
  252.3 3.3 %copy-start.18 = (f32[256,1024]{1,0:T(8,128)S(1)}, f32[256,1024]{1,0:T(8,128)}, u32[]{:S(2)}) copy-start(f32[256,1024]{1,0:T(8,128)} %get-tuple-element.75) | copy-start | bytes 3145732
  255.6 1.6 copy-start.17
Sparse Core Ops, SparseCore 0:
  106.3 145.9 all-reduce.3
